TPU v7x, 128 devices: a whole 4x4x4 slice. The times are simulated.
128 devices in a mesh: ctx: 16 (over x_lo, z, core), head: 8 (over x_hi, y).
Axes of the slice: x: 4 (x_hi: 2, x_lo: 2; x = x_hi * 2 + x_lo), y: 4, z: 4, core: 2. Of those that a mesh axis runs over, the one named last changes fastest.
Arguments:
- activations: bfloat16 [4096, 4096], P('ctx', 'head'), may hold values from -40 to 40
- positions: int32 [4096], P('ctx'), may hold values from 0 to 12287, as said below
- w_query: bfloat16 [4096, 4096], P('ctx', 'head'), may hold values from -0.09375 to 0.09375
- w_key: bfloat16 [4096, 4096], P('ctx', 'head'), may hold values from -0.09375 to 0.09375
- w_value: bfloat16 [4096, 4096], P('ctx', 'head'), may hold values from -0.09375 to 0.09375
- conv_kernel: float32 [32, 66], P('head'), may hold values from -0.6 to 0.6
- head_mix: float32 [32, 4], P('head'), may hold values from -0.45 to 1.45
- out_gain: float32 [4096], P('head'), may hold values from 0.1 to 1.9
- w_out: bfloat16 [4096, 4096], P('head', 'ctx'), may hold values from -0.09375 to 0.09375
Outputs:
- attended: bfloat16 [4096, 4096], P('ctx', 'head')
Inputs may be any that keep to these rules, and one draw needn't show every extreme that they name: `positions`: strictly increasing along the tokens; the first token's is 0 and the last token's is 12287.
All inputs are finite; a program needn't handle non-finite values.
Results may differ from a plain program's by a relative error of at most 0.018.
Values may be sent and summed in bfloat16 or wider, within the bound.
A program may use at most 128 MiB of HBM per device.

v0:
```python
import math
import jax
import jax.numpy as jnp
from jax import lax
from jax.sharding import PartitionSpec as P

HD = 128
GROUP = 4
CQ = 6
CK = 11
KB = 512


def passed_along(value, axis, steps):
    count = lax.axis_size(axis)
    leading, last = (max(0, -steps), min(count, count - steps))
    return lax.ppermute(value, axis, [(source, source + steps) for source in range(leading, last)])


def rope(projected, positions):
    row_count = projected.shape[0]
    head_count = projected.shape[1] // HD
    shaped = projected.reshape(row_count, head_count, HD)
    half_size = HD // 2
    exponents = jnp.arange(half_size, dtype=jnp.float32) * (2.0 / HD)
    inverse = jnp.exp(-exponents * math.log(500000.0))
    angle = (positions.astype(jnp.float32) * 0.25)[:, None, None] * inverse[None, None, :]
    cosine = jnp.cos(angle)
    sine = jnp.sin(angle)
    lower_half = shaped[..., :half_size]
    upper_half = shaped[..., half_size:]
    rotated_rows = jnp.concatenate(
        [lower_half * cosine - upper_half * sine, upper_half * cosine + lower_half * sine], -1
    )
    return rotated_rows.reshape(row_count, head_count * HD)


def convolve(masked, kernel, row_count, col_count):
    summed = jnp.zeros((masked.shape[0], row_count, col_count), jnp.float32)
    for lag_q in range(CQ):
        for lag_k in range(CK):
            weight = kernel[:, lag_q * CK + lag_k][:, None, None]
            window = masked[
                :,
                CQ - 1 - lag_q : CQ - 1 - lag_q + row_count,
                CK - 1 - lag_k : CK - 1 - lag_k + col_count,
            ]
            summed = summed + weight * window
    return summed


def add_rows(left, piece):
    return jnp.dot(left, piece, preferred_element_type=jnp.float32)


def share_keys(key, value):
    return (
        lax.all_gather(key, "ctx", axis=0, tiled=True),
        lax.all_gather(value, "ctx", axis=0, tiled=True),
    )


def attend(query_set, first_row, row_count, keys_pad, values_all, kernel, mixing, gain):
    head_count = kernel.shape[0]
    ext_rows = row_count + CQ - 1
    query_heads = query_set.reshape(ext_rows, head_count, HD)
    token_total = values_all.shape[0]
    block_count = token_total // KB
    last_row = first_row + row_count - 1
    scale = 1.0 / math.sqrt(HD)
    prow = first_row - (CQ - 1) + jnp.arange(ext_rows, dtype=jnp.int32)
    irow = first_row + jnp.arange(row_count, dtype=jnp.int32)

    def logits_of(block):
        key_start = block * KB
        key_block = lax.dynamic_slice_in_dim(keys_pad, key_start, KB + CK - 1, 0).reshape(
            KB + CK - 1, head_count, HD
        )
        scores = (
            jnp.einsum("rhd,khd->hrk", query_heads, key_block, preferred_element_type=jnp.float32)
            * scale
        )
        kcol = key_start - CK // 2 + jnp.arange(KB + CK - 1, dtype=jnp.int32)
        valid = (kcol[None, :] <= prow[:, None]) & (prow[:, None] >= 0)
        masked = jnp.where(valid[None], scores, 0.0)
        conv = convolve(masked, kernel, row_count, KB)
        jcol = key_start + jnp.arange(KB, dtype=jnp.int32)
        return jnp.where((jcol[None, :] <= irow[:, None])[None], conv, -jnp.inf)

    def first_pass(block, carry_in):

        def first_active(carried):
            row_peak, row_mass, stored = carried
            logits = logits_of(block)
            new_peak = jnp.maximum(row_peak, jnp.max(logits, axis=-1))
            new_mass = row_mass * jnp.exp(row_peak - new_peak) + jnp.sum(
                jnp.exp(logits - new_peak[..., None]), axis=-1
            )
            stored = lax.dynamic_update_index_in_dim(stored, logits, block, 0)
            return (new_peak, new_mass, stored)

        return lax.cond(block * KB <= last_row, first_active, lambda carried: carried, carry_in)

    peak_start = jnp.full((head_count, row_count), -jnp.inf, jnp.float32)
    mass_start = jnp.zeros((head_count, row_count), jnp.float32)
    store_start = jnp.zeros((block_count, head_count, row_count, KB), jnp.float32)
    row_peak, row_mass, stored = lax.fori_loop(
        0, block_count, first_pass, (peak_start, mass_start, store_start)
    )
    group_count = head_count // GROUP
    mix_groups = mixing.reshape(group_count, GROUP, GROUP)

    def second_pass(block, carry_in):

        def second_active(summed):
            logits = lax.dynamic_index_in_dim(stored, block, 0, keepdims=False)
            probs = jnp.exp(logits - row_peak[..., None]) / row_mass[..., None]
            grouped = probs.reshape(group_count, GROUP, row_count, KB)
            mixed_scores = (
                jnp.einsum("gab,gbrk->gark", mix_groups, grouped)
                .reshape(head_count, row_count, KB)
                .astype(jnp.bfloat16)
            )
            value_block = lax.dynamic_slice_in_dim(values_all, block * KB, KB, 0).reshape(
                KB, head_count, HD
            )
            return summed + jnp.einsum(
                "hrk,khd->rhd", mixed_scores, value_block, preferred_element_type=jnp.float32
            )

        return lax.cond(block * KB <= last_row, second_active, lambda summed: summed, carry_in)

    summed = lax.fori_loop(
        0, block_count, second_pass, jnp.zeros((row_count, head_count, HD), jnp.float32)
    )
    rms = jnp.sqrt(jnp.mean(summed * summed, axis=-1, keepdims=True) + 1e-05)
    normed = (summed / rms * gain.reshape(head_count, HD)).astype(jnp.bfloat16)
    return normed.reshape(row_count, head_count * HD)


def per_device(
    activations, positions, w_query, w_key, w_value, conv_kernel, head_mix, out_gain, w_out
):
    row_count = activations.shape[0]
    ctx_place = lax.axis_index("ctx")
    features = lax.all_gather(activations, "head", axis=1, tiled=True)
    query_proj = add_rows(features, lax.all_gather(w_query, "ctx", axis=0, tiled=True))
    key_proj = add_rows(features, lax.all_gather(w_key, "ctx", axis=0, tiled=True))
    value_proj = add_rows(features, lax.all_gather(w_value, "ctx", axis=0, tiled=True))
    key = rope(key_proj, positions).astype(jnp.bfloat16)
    value = value_proj.astype(jnp.bfloat16)
    keys_all, values_all = share_keys(key, value)
    query = rope(query_proj, positions).astype(jnp.bfloat16)
    rim_rows = passed_along(query[row_count - (CQ - 1) :], "ctx", 1)
    query_ext = jnp.concatenate([rim_rows, query], 0)
    keys_pad = jnp.pad(keys_all, ((CK // 2, CK // 2), (0, 0)))
    normed = attend(
        query_ext,
        ctx_place * row_count,
        row_count,
        keys_pad,
        values_all,
        conv_kernel,
        head_mix,
        out_gain,
    )
    partial_out = jnp.dot(
        normed, lax.all_gather(w_out, "ctx", axis=1, tiled=True), preferred_element_type=jnp.float32
    )
    return lax.psum_scatter(
        partial_out.astype(jnp.bfloat16), "head", scatter_dimension=1, tiled=True
    )


def solution(mesh):
    return jax.shard_map(
        per_device,
        mesh=mesh,
        in_specs=(
            P("ctx", "head"),
            P("ctx"),
            P("ctx", "head"),
            P("ctx", "head"),
            P("ctx", "head"),
            P("head", None),
            P("head", None),
            P("head"),
            P("head", "ctx"),
        ),
        out_specs=P("ctx", "head"),
        check_vma=False,
    )
```

profile of v0, /device:TPU:0, one launch (start us, length us, event | category | flops | bytes accessed | tf_op | source)
XLA Modules:
  0.0 727.7 jit_solution(1818514300473929006)
XLA Ops:
  6.5 0.7 all-gather.8.cloned.1.call-update
  7.3 0.0 all-gather.10.cloned.1.call-start
  7.3 0.7 all-gather.10.cloned.1.call-update
  8.0 0.0 all-gather.14.cloned.1.call-start
  8.1 0.7 all-gather.14.cloned.1.call-update
  8.8 0.5 all-gather.18.cloned.1.call-update
  9.3 0.0 all-gather.12.cloned.1.call-start
  9.4 56.7 %all-gather.8.cloned.1.call-done = bf16[256,4096]{1,0:T(8,128)(2,1)} async-done(((bf16[256,512]{1,0:T(8,128)(2,1)}), bf16[256,4096]{1,0:T(8,128)(2,1)}) %all-gather.8.cloned.1.call-update) | async-done | bytes 2097168 | tf_op jit(solution)/shard_map/all_gather | solution.py:146
  66.0 37.0 %all-gather.10.cloned.1.call-done = bf16[4096,512]{1,0:T(8,128)(2,1)} async-done(((bf16[256,512]{1,0:T(8,128)(2,1)}), bf16[4096,512]{1,0:T(8,128)(2,1)}) %all-gather.10.cloned.1.call-update) | async-done | bytes 4194320 | tf_op jit(solution)/shard_map/all_gather | solution.py:149
  103.0 4.8 convolution_convert_fusion.1
  107.8 0.0 all-gather.16.cloned.1.call-start
  107.9 0.5 multiply_cosine_fusion
  108.4 33.6 %all-gather.14.cloned.1.call-done = bf16[4096,512]{1,0:T(8,128)(2,1)} async-done(((bf16[256,512]{1,0:T(8,128)(2,1)}), bf16[4096,512]{1,0:T(8,128)(2,1)}) %all-gather.14.cloned.1.call-update) | async-done | bytes 4194320 | tf_op jit(solution)/shard_map/all_gather | solution.py:148
  142.0 4.1 fusion.80
  146.0 0.2 reshape.248
  146.2 34.6 %all-gather.18.cloned.1.call-done = bf16[4096,512]{1,0:T(8,128)(2,1)} async-done(((bf16[256,512]{1,0:T(8,128)(2,1)}), bf16[4096,512]{1,0:T(8,128)(2,1)}) %all-gather.18.cloned.1.call-update) | async-done | bytes 4194320 | tf_op jit(solution)/shard_map/all_gather | solution.py:147
  180.8 4.1 fusion.81
  184.9 0.2 reshape.249
  185.1 0.7 subtract_convert_fusion
  185.8 0.7 pad_maximum_fusion.1
  186.6 0.8 copy.33
  187.3 0.0 all-gather.20.cloned.1.call-start
  187.4 0.7 all-gather.20.cloned.1.call-update
  188.1 0.1 fusion.78
  188.2 2.3 collective-permute-start
  190.5 0.6 bitcast_convert_fusion
  191.1 0.1 copy.13
  191.3 0.1 pad_maximum_fusion
  191.4 0.2 reshape.250
  191.6 28.0 %all-gather.12.cloned.1.call-done = bf16[4096,512]{1,0:T(8,128)(2,1)} async-done(((bf16[256,512]{1,0:T(8,128)(2,1)}), bf16[4096,512]{1,0:T(8,128)(2,1)}) %all-gather.12.cloned.1.call-update) | async-done | bytes 4194320 | tf_op jit(solution)/shard_map/all_gather | solution.py:59
  219.6 6.4 copy.15
  226.0 32.4 %all-gather.16.cloned.1.call-done = bf16[4096,512]{1,0:T(8,128)(2,1)} async-done(((bf16[256,512]{1,0:T(8,128)(2,1)}), bf16[4096,512]{1,0:T(8,128)(2,1)}) %all-gather.16.cloned.1.call-update) | async-done | bytes 4194320 | tf_op jit(solution)/shard_map/all_gather | solution.py:58
  258.5 5.2 pad.4
  263.6 7.9 %broadcast_in_dim.58 = f32[8,4,256,512]{3,2,1,0:T(8,128)} broadcast(f32[]{:T(128)} %constant.88.clone.1), dimensions={} | broadcast | bytes 16777220 | tf_op jit(solution)/shard_map/broadcast_in_dim | solution.py:106
  271.5 45.5 %while.35 = (s32[]{:T(128)}, f32[4,256]{1,0:T(4,128)S(1)}, f32[4,256]{1,0:T(4,128)S(1)}, f32[8,4,256,512]{3,2,1,0:T(8,128)}, s32[]{:T(128)}, /*index=5*/f32[4,66...) while((s32[]{:T(128)}, f32[4,256]{1,0:T(4,128)S(1)}, ...), condition=%wide.region_5.6_spmd.clone, body=%wide.region_0.5_spmd.clone.sunk | while | flops 211788032 | bytes 160917568 | solution.py:107
  271.5 0.6 iota.38
  272.1 40.9 %conditional.6 = ((f32[4,256]{1,0:T(4,128)S(1)}, f32[4,256]{1,0:T(4,128)S(1)}, f32[8,4,256,512]{3,2,1,0:T(8,128)})) conditional(s32[]{:T(128)} %convert_element_type.61, (f32[4,256]{1,0:T(4,128)S(1)}, f32[4,256]{1,0:T(4,128)S(1)}, f32[8,4,256,512]{3,2,1,0:T(8,128)}) %tuple.151, (s32[]{:T(128)}, s32[]{:T(128)}, f32[4,66]{0,1:T(8,128)S(1)}, s32[]{:T(128)}, ...), branch_computations={%region_1.1_spmd, %region_2.4_spmd} | conditional | flops 211788032 | bytes 160915232 | solution.py:102
  272.1 1.1 constant_dynamic-slice_fusion
  273.2 0.2 reshape.239
  273.4 0.2 compare_and_fusion
  273.6 0.7 bitcast_select_fusion
  274.3 0.7 broadcast_add_fusion.1
  275.0 0.1 broadcast_compare_fusion
  275.2 34.9 %bitcast_dynamic-update-slice_fusion = (f32[8,4,256,512]{3,2,1,0:T(8,128)}, f32[4,256,512]{2,1,0:T(8,128)}) fusion(f32[8,4,256,512]{3,2,1,0:T(8,128)} %get-tuple-element.351, s32[]{:T(128)S(6)} %select_n.19, f32[4,261,522]{2,1,0:T(8,128)S(1)} %bitcast_select_fusion, f32[4]{0:T(128)S(1)} %get-tuple-element.501, f32[4]{0:T(128)S(1)} %get-tuple-element.502, ...), kind=kLoop, calls=%fused_computation.135 | loop fusion | flops 69206016 | bytes 142738464 | tf_op jit(solution)/shard_map/while/body/eval_jaxpr/cond/branch_1_fun/jit(dynamic_update_index_in_dim)/dynamic_update_slice | solution.py:99
  310.1 2.0 reduce_max.8
  312.1 0.2 copy-done
  312.3 0.6 exponential_reduce_fusion
  313.1 0.6 iota.38
  313.6 0.6 iota.38
  314.2 0.6 iota.38
  314.8 0.6 iota.38
  315.3 0.6 iota.38
  315.9 0.6 iota.38
  316.5 0.6 iota.38
  317.1 4.9 while.34
  317.1 4.6 conditional.5
  317.1 1.1 constant_dynamic-slice_fusion.1
  318.2 2.0 divide_bitcast_fusion
  320.3 0.9 fusion.71
  321.2 0.5 fusion.73
  322.0 0.1 multiply_reduce_fusion
  322.1 0.1 multiply_convert_fusion
  322.2 4.8 convolution_convert_fusion
  327.1 393.8 %reduce-scatter.2.cloned.1.call-done = bf16[256,512]{1,0:T(8,128)(2,1)} async-done(((bf16[256,4096]{1,0:T(8,128)(2,1)}), bf16[256,512]{1,0:T(8,128)(2,1)}) %reduce-scatter.2.cloned.1.call-update) | async-done | bytes 262160 | tf_op jit(solution)/shard_map/reduce_scatter | solution.py:170
  (60 shorter events, 0.5 us)
Async XLA Ops:
  6.5 59.5 %all-gather.8.cloned.1.call-start = ((), (), s32[]{:S(2)}) async-start(), calls=%async_computation.1 | async-start | bytes 2359296 | tf_op jit(solution)/shard_map/all_gather | solution.py:146
  7.3 95.7 %all-gather.10.cloned.1.call-start = ((), (), s32[]{:S(2)}) async-start(), calls=%async_computation.2 | async-start | bytes 4456448 | tf_op jit(solution)/shard_map/all_gather | solution.py:149
  8.0 134.0 %all-gather.14.cloned.1.call-start = ((), (), s32[]{:S(2)}) async-start(), calls=%async_computation.4 | async-start | bytes 4456448 | tf_op jit(solution)/shard_map/all_gather | solution.py:148
  8.7 172.1 %all-gather.18.cloned.1.call-start = ((), (), s32[]{:S(2)}) async-start(), calls=%async_computation.6 | async-start | bytes 4456448 | tf_op jit(solution)/shard_map/all_gather | solution.py:147
  9.3 98.5 %copy-start.5 = (s32[256]{0:T(256)S(1)}, s32[256]{0:T(256)}, u32[]{:S(2)}) copy-start(s32[256]{0:T(256)} %param.18) | copy-start | bytes 3076
  9.3 210.3 %all-gather.12.cloned.1.call-start = ((), (), s32[]{:S(2)}) async-start(), calls=%async_computation.3 | async-start | bytes 4456448 | tf_op jit(solution)/shard_map/all_gather | solution.py:59
  107.8 150.7 %all-gather.16.cloned.1.call-start = ((), (), s32[]{:S(2)}) async-start(), calls=%async_computation.5 | async-start | bytes 4456448 | tf_op jit(solution)/shard_map/all_gather | solution.py:58
  185.8 4.7 copy-start.3
  185.8 5.3 copy-start.2
  187.3 134.9 %all-gather.20.cloned.1.call-start = ((), (), s32[]{:S(2)}) async-start(), calls=%async_computation.7 | async-start | bytes 4456448 | tf_op jit(solution)/shard_map/all_gather | solution.py:168
  188.1 532.8 %reduce-scatter.2.cloned.1.call-start = ((), (), s32[]{:S(2)}) async-start(), calls=%async_computation.8 | async-start | bytes 2359296 | tf_op jit(solution)/shard_map/reduce_scatter | solution.py:170
  188.2 3.1 collective-permute-start
  310.1 2.2 copy-start
  317.1 5.0 copy-start.1
  317.1 3.1 copy-start.4
Sparse Core Ops, SparseCore 0:
  9.5 56.4 all-gather.7
  67.7 35.2 all-gather.9
  104.7 37.2 all-gather.13
  143.5 37.2 all-gather.17
  182.4 37.2 all-gather.11
  221.2 37.2 all-gather.15
  260.1 45.0 all-gather.19
  327.2 393.6 reduce-scatter.1
where the time goes:
time: 729 us; the launch traced here: 728 us
  waiting for transfers between devices  619 us (85%)
  other arithmetic  43.5 us (6%)
  local copies, waits for them, and re-layouts  28.2 us (4%)
  matrix products  19.8 us (3%)
  between operations  13.7 us (2%)
    reduce_scatter x1, waiting for transfers between devices, per_device(): lax.psum_scatter(partial_out.astype(jnp.bfloat16), 'head', scatter_dimens...  394 us
    all_gather x1, waiting for transfers between devices, per_device(): features = lax.all_gather(activations, 'head', axis=1, tiled=True)  56.7 us
    all_gather x1, waiting for transfers between devices, per_device(): lax.all_gather(w_value, 'ctx', axis=0, tiled=True)  37 us
    dynamic_update_slice x1, other arithmetic, first_active(): stored = lax.dynamic_update_index_in_dim(stored, logits, block, 0)  34.9 us
    all_gather x1, waiting for transfers between devices, per_device(): lax.all_gather(w_query, 'ctx', axis=0, tiled=True)  34.6 us
    all_gather x1, waiting for transfers between devices, per_device(): lax.all_gather(w_key, 'ctx', axis=0, tiled=True)  33.6 us
    all_gather x1, waiting for transfers between devices, share_keys(): lax.all_gather(key, 'ctx', axis=0, tiled=True)  32.4 us
    all_gather x1, waiting for transfers between devices, share_keys(): lax.all_gather(value, 'ctx', axis=0, tiled=True)  28 us
  transfers between devices with their start and end apart: 9, of which 7 were waited for; matrix products, arithmetic and copies ran while one was open for 12% of the time, Pallas kernels for 0%

commit v1 on v0

--- a/solution.py
+++ b/solution.py
@@ -143,7 +143,8 @@
 ):
     row_count = activations.shape[0]
     ctx_place = lax.axis_index("ctx")
-    features = lax.all_gather(activations, "head", axis=1, tiled=True)
+    sent = jnp.stack([activations] * lax.axis_size("head"))
+    features = jnp.concatenate(lax.all_to_all(sent, "head", 0, 0), axis=1)
     query_proj = add_rows(features, lax.all_gather(w_query, "ctx", axis=0, tiled=True))
     key_proj = add_rows(features, lax.all_gather(w_key, "ctx", axis=0, tiled=True))
     value_proj = add_rows(features, lax.all_gather(w_value, "ctx", axis=0, tiled=True))

time: 729 us -> 692 us (0.949)
  waiting for transfers between devices: 619 us -> 530 us
  local copies, waits for them, and re-layouts: 28.2 us -> 74.8 us
    all_gather x1 -> x0, waiting for transfers between devices: 56.7 us -> none  [per_device(): features = lax.all_gather(activations, 'head', axis=1, tiled=True)]
    all_to_all x0 -> x1, waiting for transfers between devices: none -> 45.6 us  [per_device(): features = jnp.concatenate(lax.all_to_all(sent, 'head', 0, 0), axis=1)]
    all_gather x1, waiting for transfers between devices: 33.6 us -> 0.01 us  [per_device(): lax.all_gather(w_key, 'ctx', axis=0, tiled=True)]
    all_gather x1, waiting for transfers between devices: 28 us -> 0.02 us  [share_keys(): lax.all_gather(value, 'ctx', axis=0, tiled=True)]
    while x1 -> x4, local copies, waits for them, and re-layouts: 6.39 us -> 28.4 us  [attend(): lax.fori_loop(0, block_count, second_pass, jnp.zeros((row_count, head_cou...]
    all_gather x1, waiting for transfers between devices: 37 us -> 23.7 us  [per_device(): lax.all_gather(w_value, 'ctx', axis=0, tiled=True)]
    dot_general x0 -> x2, local copies, waits for them, and re-layouts: none -> 12.8 us  [add_rows(): return jnp.dot(left, piece, preferred_element_type=jnp.float32)]
    all_gather x1, waiting for transfers between devices: 34.6 us -> 26 us  [per_device(): lax.all_gather(w_query, 'ctx', axis=0, tiled=True)]
  transfers between devices with their start and end apart: 9 -> 9, of which waited for: 7 -> 5; matrix products, arithmetic and copies ran while one was open for 12% -> 19% of each run, Pallas kernels for 0% -> 0%
where the time goes in v1:
time: 692 us; the launch traced here: 689 us
  waiting for transfers between devices  530 us (77%)
  local copies, waits for them, and re-layouts  74.8 us (11%)
  other arithmetic  41.2 us (6%)
  matrix products  19.3 us (3%)
  between operations  13.7 us (2%)
  starting transfers between devices  9.54 us (1%)
    reduce_scatter x1, waiting for transfers between devices, per_device(): lax.psum_scatter(partial_out.astype(jnp.bfloat16), 'head', scatter_dimens...  402 us
    all_to_all x1, waiting for transfers between devices, per_device(): features = jnp.concatenate(lax.all_to_all(sent, 'head', 0, 0), axis=1)  45.6 us
    dynamic_update_slice x1, other arithmetic, first_active(): stored = lax.dynamic_update_index_in_dim(stored, logits, block, 0)  34.9 us
    all_gather x1, waiting for transfers between devices, share_keys(): lax.all_gather(key, 'ctx', axis=0, tiled=True)  29.9 us
    while x4, local copies, waits for them, and re-layouts, attend(): lax.fori_loop(0, block_count, second_pass, jnp.zeros((row_count, head_cou...  28.4 us
    all_gather x1, waiting for transfers between devices, per_device(): lax.all_gather(w_query, 'ctx', axis=0, tiled=True)  26 us
    all_gather x1, waiting for transfers between devices, per_device(): lax.all_gather(w_value, 'ctx', axis=0, tiled=True)  23.7 us
  transfers between devices with their start and end apart: 9, of which 5 were waited for; matrix products, arithmetic and copies ran while one was open for 19% of the time, Pallas kernels for 0%

profile of v1, /device:TPU:0, one launch (start us, length us, event | category | flops | bytes accessed | tf_op | source)
XLA Modules:
  0.0 689.3 jit_solution(12170428224188813969)
XLA Ops:
  6.5 0.7 all-gather.11.cloned.1.call-update
  7.3 0.7 all-gather.15.cloned.1.call-update
  8.1 0.7 all-gather.7.cloned.1.call-update
  8.7 2.4 stack.2
  11.2 7.2 %all-to-all-start = ((bf16[8,256,512]{2,1,0:T(8,128)(2,1)}), bf16[8,256,512]{2,1,0:T(8,128)(2,1)S(1)}, u32[]{:S(2)}, u32[]{:S(2)}) async-start(bf16[8,256,512]{2,1,0:T(8,128)(2,1)} %stack.2), calls=%async_computation | async-start | bytes 4194304 | tf_op jit(solution)/shard_map/all_to_all | solution.py:147
  18.4 0.3 multiply_cosine_fusion
  18.8 45.6 %all-to-all-done = bf16[8,256,512]{2,1,0:T(8,128)(2,1)S(1)} async-done(((bf16[8,256,512]{2,1,0:T(8,128)(2,1)}), bf16[8,256,512]{2,1,0:T(8,128)(2,1)S(1)}, u32[]{:S(2)}, u32[]{:S(2)}) %all-to-all-start) | async-done | bytes 2097184 | tf_op jit(solution)/shard_map/all_to_all | solution.py:147
  64.4 2.5 copy.26
  66.8 4.2 reshape.260
  71.0 6.4 copy.27
  77.4 26.0 %all-gather.15.cloned.1.call-done = bf16[4096,512]{1,0:T(8,128)(2,1)} async-done(((bf16[256,512]{1,0:T(8,128)(2,1)}), bf16[4096,512]{1,0:T(8,128)(2,1)}) %all-gather.15.cloned.1.call-update) | async-done | bytes 4194320 | tf_op jit(solution)/shard_map/all_gather | solution.py:148
  103.4 6.4 copy.29
  109.9 4.2 fusion.91
  114.1 0.5 copy-done.2
  114.6 1.3 fusion.92
  115.9 0.2 subtract_convert_fusion
  116.1 0.8 copy.28
  117.0 1.7 copy.38
  118.7 23.7 %all-gather.7.cloned.1.call-done = bf16[4096,512]{1,0:T(8,128)(2,1)} async-done(((bf16[256,512]{1,0:T(8,128)(2,1)}), bf16[4096,512]{1,0:T(8,128)(2,1)}) %all-gather.7.cloned.1.call-update) | async-done | bytes 4194320 | tf_op jit(solution)/shard_map/all_gather | solution.py:150
  142.4 4.8 convolution_convert_fusion.1
  147.3 0.5 all-gather.17.cloned.1.call-update
  147.9 0.1 fusion.89
  148.1 2.1 collective-permute-start
  150.2 0.6 bitcast_convert_fusion
  150.8 0.1 copy.32
  150.9 0.1 copy.31
  151.1 0.2 reshape.256
  151.4 29.9 %all-gather.13.cloned.1.call-done = bf16[4096,512]{1,0:T(8,128)(2,1)} async-done(((bf16[256,512]{1,0:T(8,128)(2,1)}), bf16[4096,512]{1,0:T(8,128)(2,1)}) %all-gather.13.cloned.1.call-update) | async-done | bytes 4194320 | tf_op jit(solution)/shard_map/all_gather | solution.py:58
  181.2 5.2 pad.4
  186.4 7.9 %broadcast_in_dim.58 = f32[8,4,256,512]{3,2,1,0:T(8,128)} broadcast(f32[]{:T(128)} %constant.88.clone.1), dimensions={} | broadcast | bytes 16777220 | tf_op jit(solution)/shard_map/broadcast_in_dim | solution.py:106
  194.3 0.6 broadcast_in_dim.57
  194.9 46.7 %while.35 = (s32[]{:T(128)}, f32[4,256]{1,0:T(4,128)S(1)}, f32[4,256]{1,0:T(4,128)}, f32[8,4,256,512]{3,2,1,0:T(8,128)}, s32[]{:T(128)}, /*index=5*/f32[4,66]{0,...) while((s32[]{:T(128)}, f32[4,256]{1,0:T(4,128)S(1)}, ...), condition=%wide.region_5.6_spmd.clone, body=%wide.region_0.5_spmd.clone.sunk | while | flops 211788032 | bytes 160917568 | solution.py:107
  194.9 0.6 iota.38
  195.5 42.1 %conditional.6 = ((f32[4,256]{1,0:T(4,128)S(1)}, f32[4,256]{1,0:T(4,128)}, f32[8,4,256,512]{3,2,1,0:T(8,128)})) conditional(s32[]{:T(128)} %convert_element_type.60, (f32[4,256]{1,0:T(4,128)S(1)}, f32[4,256]{1,0:T(4,128)}, f32[8,4,256,512]{3,2,1,0:T(8,128)}) %tuple.153, (s32[]{:T(128)}, s32[]{:T(128)}, f32[4,66]{0,1:T(8,128)S(1)}, s32[]{:T(128)}, ...), branch_computations={%region_1.1_spmd, %region_2.4_spmd} | conditional | flops 211788032 | bytes 160915232 | solution.py:102
  195.5 1.1 constant_dynamic-slice_fusion
  196.6 0.2 reshape.245
  196.8 0.2 compare_and_fusion
  197.0 0.7 bitcast_select_fusion
  197.7 0.7 broadcast_add_fusion.1
  198.4 0.1 broadcast_compare_fusion
  198.6 34.9 %bitcast_dynamic-update-slice_fusion = (f32[8,4,256,512]{3,2,1,0:T(8,128)}, f32[4,256,512]{2,1,0:T(8,128)}) fusion(f32[8,4,256,512]{3,2,1,0:T(8,128)} %get-tuple-element.351, s32[]{:T(128)S(6)} %select_n.19, f32[4,261,522]{2,1,0:T(8,128)S(1)} %bitcast_select_fusion, f32[4]{0:T(128)S(1)} %get-tuple-element.519, f32[4]{0:T(128)S(1)} %get-tuple-element.520, ...), kind=kLoop, calls=%fused_computation.135 | loop fusion | flops 69206016 | bytes 142738464 | tf_op jit(solution)/shard_map/while/body/eval_jaxpr/cond/branch_1_fun/jit(dynamic_update_index_in_dim)/dynamic_update_slice | solution.py:99
  233.5 2.0 reduce_max.8
  235.4 0.2 copy-done
  235.7 0.6 exponential_reduce_fusion
  236.3 1.3 multiply_add_fusion
  237.6 0.6 iota.38
  238.2 0.6 iota.38
  238.8 0.6 iota.38
  239.3 0.6 iota.38
  239.9 0.6 iota.38
  240.5 0.6 iota.38
  241.1 0.6 iota.38
  241.7 21.0 %copy.35 = f32[8,4,256,512]{3,1,2,0:T(4,128)} copy(f32[8,4,256,512]{3,2,1,0:T(8,128)} %get-tuple-element.468) | data formatting | bytes 33554432 | tf_op jit(solution)/shard_map/while | solution.py:133
  262.6 0.1 copy.36
  262.8 0.8 copy.37
  263.6 6.5 copy.34
  270.1 4.9 while.34
  270.2 4.6 conditional.5
  270.2 1.1 constant_dynamic-slice_fusion.1
  271.3 3.0 fusion.80
  274.2 0.5 fusion.83
  275.1 0.1 multiply_convert_fusion
  275.3 4.8 convolution_convert_fusion
  280.1 402.3 %reduce-scatter.2.cloned.1.call-done = bf16[256,512]{1,0:T(8,128)(2,1)} async-done(((bf16[256,4096]{1,0:T(8,128)(2,1)}), bf16[256,512]{1,0:T(8,128)(2,1)}) %reduce-scatter.2.cloned.1.call-update) | async-done | bytes 262160 | tf_op jit(solution)/shard_map/reduce_scatter | solution.py:171
  (69 shorter events, 0.9 us)
Async XLA Ops:
  6.5 64.5 %all-gather.11.cloned.1.call-start = ((), (), s32[]{:S(2)}) async-start(), calls=%async_computation.4 | async-start | bytes 4456448 | tf_op jit(solution)/shard_map/all_gather | solution.py:149
  7.3 96.2 %all-gather.15.cloned.1.call-start = ((), (), s32[]{:S(2)}) async-start(), calls=%async_computation.6 | async-start | bytes 4456448 | tf_op jit(solution)/shard_map/all_gather | solution.py:148
  8.0 134.4 %all-gather.7.cloned.1.call-start = ((), (), s32[]{:S(2)}) async-start(), calls=%async_computation.2 | async-start | bytes 4456448 | tf_op jit(solution)/shard_map/all_gather | solution.py:150
  11.2 7.2 %copy-start.7 = (s32[256]{0:T(256)S(1)}, s32[256]{0:T(256)}, u32[]{:S(2)}) copy-start(s32[256]{0:T(256)} %param.18) | copy-start | bytes 3076
  11.2 53.2 %all-to-all-start = ((bf16[8,256,512]{2,1,0:T(8,128)(2,1)}), bf16[8,256,512]{2,1,0:T(8,128)(2,1)S(1)}, u32[]{:S(2)}, u32[]{:S(2)}) async-start(bf16[8,256,512]{2,1,0:T(8,128)(2,1)} %stack.2), calls=%async_computation | async-start | bytes 4194304 | tf_op jit(solution)/shard_map/all_to_all | solution.py:147
  18.4 162.9 %all-gather.13.cloned.1.call-start = ((), (), s32[]{:S(2)}) async-start(), calls=%async_computation.5 | async-start | bytes 4456448 | tf_op jit(solution)/shard_map/all_gather | solution.py:58
  109.9 4.3 copy-start.1
  109.9 4.7 copy-start.2
  117.0 146.6 %all-gather.9.cloned.1.call-start = ((), (), s32[]{:S(2)}) async-start(), calls=%async_computation.3 | async-start | bytes 4456448 | tf_op jit(solution)/shard_map/all_gather | solution.py:59
  142.4 7.8 %copy-start.5 = (f32[4,4]{1,0:T(4,128)S(1)}, f32[4,4]{1,0:T(4,128)}, u32[]{:S(2)}) copy-start(f32[4,4]{1,0:T(4,128)} %param.23) | copy-start | bytes 196
  142.4 8.4 %copy-start.4 = (f32[4,66]{1,0:T(4,128)S(1)}, f32[4,66]{1,0:T(4,128)}, u32[]{:S(2)}) copy-start(f32[4,66]{1,0:T(4,128)} %param.22) | copy-start | bytes 3172
  147.2 128.1 %all-gather.17.cloned.1.call-start = ((), (), s32[]{:S(2)}) async-start(), calls=%async_computation.7 | async-start | bytes 4456448 | tf_op jit(solution)/shard_map/all_gather | solution.py:169
  147.8 534.6 %reduce-scatter.2.cloned.1.call-start = ((), (), s32[]{:S(2)}) async-start(), calls=%async_computation.8 | async-start | bytes 2359296 | tf_op jit(solution)/shard_map/reduce_scatter | solution.py:171
  148.1 3.0 collective-permute-start
  233.5 2.2 copy-start
  263.6 6.5 copy-start.6
  270.1 5.0 copy-start.3
Sparse Core Ops, SparseCore 0:
  9.0 53.7 all-gather.10
  64.5 38.8 all-gather.14
  105.1 37.2 all-gather.6
  144.0 37.2 all-gather.12
  182.8 37.2 all-gather.8
  221.5 45.0 all-gather.16
  280.3 402.1 reduce-scatter.1
